TPU v7x, 32 devices: a whole 2x2x4 slice. The times are simulated.
32 devices in a mesh: wide: 8 (over y, x, core), narrow: 4 (over z).
Axes of the slice: x: 2, y: 2, z: 4, core: 2. Of those that a mesh axis runs over, the one named last changes fastest.
Arguments:
- query_tokens: bfloat16 [4096, 768], P(('wide', 'narrow')), may hold values from -6 to 6
- passage_tokens: bfloat16 [12288, 768], P(('wide', 'narrow')), may hold values from -6 to 6
- query_cotangent: bfloat16 [4096, 768], P(('wide', 'narrow')), may hold values from -6 to 6
- passage_cotangent: bfloat16 [12288, 768], P(('wide', 'narrow')), may hold values from -6 to 6
- query_segments: int32 [8, 512], P('wide'), may hold values from -1 to 15, as said below
- passage_segments: int32 [24, 512], P('wide'), may hold values from -1 to 3, as said below
- query_cls: int32 [8, 16], P('wide'), may hold values from 0 to 485, as said below
- passage_cls: int32 [24, 4], P('wide'), may hold values from 0 to 485, as said below
- query_weight: bfloat16 [2, 768, 768], P(None, None, 'narrow'), may hold values from -0.3125 to 0.3125
- query_bias: float32 [2, 768], P(None, 'narrow'), may hold values from -3 to 3
- key_weight: bfloat16 [2, 768, 768], P(None, None, 'narrow'), may hold values from -0.3125 to 0.3125
- value_weight: bfloat16 [2, 768, 768], P(None, None, 'narrow'), may hold values from -0.21875 to 0.21875
- value_bias: float32 [2, 768], P(None, 'narrow'), may hold values from -3 to 3
- out_weight: bfloat16 [2, 768, 768], P(None, 'narrow'), may hold values from -1.25 to 1.25
- out_bias: float32 [2, 768], replicated, may hold values from -3 to 3
- norm1_gain: float32 [2, 768], replicated, may hold values from 0.25 to 1.75
- norm1_bias: float32 [2, 768], replicated, may hold values from -3 to 3
- inner_weight: bfloat16 [2, 768, 3072], P(None, None, 'narrow'), may hold values from -0.21875 to 0.21875
- inner_bias: float32 [2, 3072], P(None, 'narrow'), may hold values from -3 to 3
- outer_weight: bfloat16 [2, 3072, 768], P(None, 'narrow'), may hold values from -0.109375 to 0.109375
- outer_bias: float32 [2, 768], replicated, may hold values from -3 to 3
- norm2_gain: float32 [2, 768], replicated, may hold values from 0.25 to 1.75
- norm2_bias: float32 [2, 768], replicated, may hold values from -3 to 3
Outputs:
- query_out: bfloat16 [4096, 768], P(('wide', 'narrow'))
- passage_out: bfloat16 [12288, 768], P(('wide', 'narrow'))
- query_grad_in: bfloat16 [4096, 768], P(('wide', 'narrow'))
- passage_grad_in: bfloat16 [12288, 768], P(('wide', 'narrow'))
- query_pooled: bfloat16 [8, 16, 768], P('wide', None, 'narrow')
- passage_pooled: bfloat16 [24, 4, 768], P('wide', None, 'narrow')
- grad_query_weight: float32 [2, 768, 768], P(None, None, 'narrow')
- grad_query_bias: float32 [2, 768], P(None, 'narrow')
- grad_key_weight: float32 [2, 768, 768], P(None, None, 'narrow')
- grad_value_weight: float32 [2, 768, 768], P(None, None, 'narrow')
- grad_value_bias: float32 [2, 768], P(None, 'narrow')
- grad_out_weight: float32 [2, 768, 768], P(None, 'narrow')
- grad_out_bias: float32 [2, 768], replicated
- grad_norm1_gain: float32 [2, 768], replicated
- grad_norm1_bias: float32 [2, 768], replicated
- grad_inner_weight: float32 [2, 768, 3072], P(None, None, 'narrow')
- grad_inner_bias: float32 [2, 3072], P(None, 'narrow')
- grad_outer_weight: float32 [2, 3072, 768], P(None, 'narrow')
- grad_outer_bias: float32 [2, 768], replicated
- grad_norm2_gain: float32 [2, 768], replicated
- grad_norm2_bias: float32 [2, 768], replicated
Inputs may be any that keep to these rules, and one draw needn't show every extreme that they name: `query_segments`: segment numbers never fall along a row and rise by one from 0 at each segment's first token; every segment spans 2 or more tokens; -1 marks padding at the end of every row. `passage_segments`: as for query_segments. query_cls[r, j] is the first position of segment j in row r of query_segments. passage_cls[r, j] is the first position of segment j in row r of passage_segments.
All inputs are finite; a program needn't handle non-finite values.
Results may differ from a plain program's by a relative error of at most 0.018.
The roundings to bfloat16 on the way count: a program that leaves them out, or rounds other values in their place, can miss the bound.
Values may be sent and summed in bfloat16 or wider, within the bound.
No kernel may reach another device: no remote copies, remote signals or barrier semaphores. Data moves between devices by JAX's collectives and lax.ppermute only.
A program may use at most 128 MiB of HBM per device.

v0:
```python
import math
import jax
import jax.numpy as jnp
from jax import lax
from jax.sharding import PartitionSpec as P

HDIM = 64
NORM_EPS = 1e-05
MASKED = -1e30


def matmul(left, right):
    return jnp.dot(left, right, preferred_element_type=jnp.float32)


def matmul_left(left, right):
    return lax.dot_general(
        left, right, (((0,), (0,)), ((), ())), preferred_element_type=jnp.float32
    )


def matmul_right(left, right):
    return lax.dot_general(
        left, right, (((1,), (1,)), ((), ())), preferred_element_type=jnp.float32
    )


def layer_norm(values, gain, bias):
    centred = values - jnp.mean(values, -1, keepdims=True)
    inverse = lax.rsqrt(jnp.mean(centred * centred, -1, keepdims=True) + NORM_EPS)
    normed = centred * inverse
    return (normed * gain + bias, normed, inverse)


def norm_back(upstream, normed, inverse, gain):
    scaled = upstream * gain
    return inverse * (
        scaled
        - jnp.mean(scaled, -1, keepdims=True)
        - normed * jnp.mean(scaled * normed, -1, keepdims=True)
    )


def gelu_slope(values):
    return 0.5 * (1.0 + lax.erf(values * (1.0 / math.sqrt(2.0)))) + values * jnp.exp(
        -0.5 * values * values
    ) * (1.0 / math.sqrt(2.0 * math.pi))


def counted(labels):
    return ((labels[:, None] == labels[None, :]) & (labels[None, :] >= 0))[None]


def attend(block, scaling):
    queries, key_vecs, value_vecs, labels = block
    scores = (
        jnp.einsum("qhd,khd->hqk", queries, key_vecs, preferred_element_type=jnp.float32) * scaling
    )
    allowed = counted(labels)
    row_top = jnp.max(jnp.where(allowed, scores, MASKED), -1, keepdims=True)
    unnorm = jnp.exp(jnp.where(allowed, scores - row_top, MASKED))
    totals = jnp.maximum(jnp.sum(unnorm, -1, keepdims=True), 1.0)
    probs = (unnorm / totals).astype(jnp.bfloat16)
    attended = jnp.einsum("hqk,khd->qhd", probs, value_vecs, preferred_element_type=jnp.float32)
    return (attended, row_top + jnp.log(totals))


def attend_back(block, scaling):
    queries, key_vecs, value_vecs, labels, log_total, upstream = block
    scores = (
        jnp.einsum("qhd,khd->hqk", queries, key_vecs, preferred_element_type=jnp.float32) * scaling
    )
    allowed = counted(labels)
    probs = jnp.exp(jnp.where(allowed, scores - log_total, MASKED))
    grad_value = jnp.einsum(
        "hqk,qhd->khd", probs.astype(jnp.bfloat16), upstream, preferred_element_type=jnp.float32
    )
    grad_probs = jnp.einsum(
        "qhd,khd->hqk", upstream, value_vecs, preferred_element_type=jnp.float32
    )
    grad_scores = (probs * (grad_probs - jnp.sum(probs * grad_probs, -1, keepdims=True))).astype(
        jnp.bfloat16
    )
    grad_query = (
        jnp.einsum("hqk,khd->qhd", grad_scores, key_vecs, preferred_element_type=jnp.float32)
        * scaling
    )
    grad_key = (
        jnp.einsum("hqk,qhd->khd", grad_scores, queries, preferred_element_type=jnp.float32)
        * scaling
    )
    return (grad_query, grad_key, grad_value)


def tower(tokens, cotangent, labels, cls_pos, weights, tower_index):
    (
        query_weight,
        query_bias,
        key_weight,
        value_weight,
        value_bias,
        out_weight,
        out_bias,
        norm1_gain,
        norm1_bias,
        inner_weight,
        inner_bias,
        outer_weight,
        outer_bias,
        norm2_gain,
        norm2_bias,
    ) = [member[tower_index] for member in weights]
    shard_rows = tokens.shape[0]
    seq_count, length = labels.shape
    head_cols = query_weight.shape[1]
    heads_here = head_cols // HDIM
    scaling = HDIM ** (-0.5)
    split_shape = (seq_count, length, heads_here, HDIM)
    full_rows = lax.all_gather(tokens, "narrow", axis=0, tiled=True)
    joined = jnp.concatenate([query_weight, key_weight, value_weight], 1)
    projected = matmul(full_rows, joined)
    queries = (projected[:, :head_cols] + query_bias).astype(jnp.bfloat16).reshape(split_shape)
    key_vecs = projected[:, head_cols : 2 * head_cols].astype(jnp.bfloat16).reshape(split_shape)
    value_vecs = (
        (projected[:, 2 * head_cols :] + value_bias).astype(jnp.bfloat16).reshape(split_shape)
    )
    attended, log_total = lax.map(
        lambda block: attend(block, scaling), (queries, key_vecs, value_vecs, labels)
    )
    attended = attended.reshape(-1, head_cols).astype(jnp.bfloat16)
    attn_out = lax.psum_scatter(
        matmul(attended, out_weight), "narrow", scatter_dimension=0, tiled=True
    )
    hidden1, normed1, inverse1 = layer_norm(
        tokens.astype(jnp.float32) + attn_out + out_bias, norm1_gain, norm1_bias
    )
    hidden_full = lax.all_gather(hidden1.astype(jnp.bfloat16), "narrow", axis=0, tiled=True)
    inner_pre = matmul(hidden_full, inner_weight) + inner_bias
    activated = jax.nn.gelu(inner_pre, approximate=False).astype(jnp.bfloat16)
    ffn_out = lax.psum_scatter(
        matmul(activated, outer_weight), "narrow", scatter_dimension=0, tiled=True
    )
    result, normed2, inverse2 = layer_norm(hidden1 + ffn_out + outer_bias, norm2_gain, norm2_bias)
    result = result.astype(jnp.bfloat16)
    cls_tokens = (cls_pos + jnp.arange(seq_count, dtype=jnp.int32)[:, None] * length).reshape(-1)
    here_rows = lax.axis_index("narrow") * shard_rows + jnp.arange(shard_rows, dtype=jnp.int32)
    picked = (cls_tokens[:, None] == here_rows[None, :]).astype(jnp.bfloat16)
    pooled_part = matmul(picked, result).reshape(seq_count, cls_pos.shape[1], -1)
    pooled = lax.psum_scatter(
        pooled_part.astype(jnp.bfloat16), "narrow", scatter_dimension=2, tiled=True
    )
    cot_rows = cotangent.astype(jnp.float32)
    grad_gain2 = jnp.sum(cot_rows * normed2, 0)
    grad_bias2 = jnp.sum(cot_rows, 0)
    grad_resid2 = norm_back(cot_rows, normed2, inverse2, norm2_gain)
    grad_outer_bias = jnp.sum(grad_resid2, 0)
    resid2_full = lax.all_gather(grad_resid2.astype(jnp.bfloat16), "narrow", axis=0, tiled=True)
    grad_outer_weight = matmul_left(activated, resid2_full)
    grad_act = matmul_right(resid2_full, outer_weight)
    grad_inner = (grad_act * gelu_slope(inner_pre)).astype(jnp.bfloat16)
    grad_inner_weight = matmul_left(hidden_full, grad_inner)
    grad_inner_bias = jnp.sum(grad_inner, 0, dtype=jnp.float32)
    grad_hidden1 = (
        lax.psum_scatter(
            matmul_right(grad_inner, inner_weight), "narrow", scatter_dimension=0, tiled=True
        )
        + grad_resid2
    )
    grad_gain1 = jnp.sum(grad_hidden1 * normed1, 0)
    grad_bias1 = jnp.sum(grad_hidden1, 0)
    grad_resid1 = norm_back(grad_hidden1, normed1, inverse1, norm1_gain)
    grad_out_bias = jnp.sum(grad_resid1, 0)
    resid1_full = lax.all_gather(grad_resid1.astype(jnp.bfloat16), "narrow", axis=0, tiled=True)
    grad_out_weight = matmul_left(attended, resid1_full)
    grad_attended = matmul_right(resid1_full, out_weight).astype(jnp.bfloat16).reshape(split_shape)
    grad_query, grad_key, grad_value = lax.map(
        lambda block: attend_back(block, scaling),
        (queries, key_vecs, value_vecs, labels, log_total, grad_attended),
    )
    grad_proj = jnp.concatenate(
        [
            grad_query.reshape(-1, head_cols),
            grad_key.reshape(-1, head_cols),
            grad_value.reshape(-1, head_cols),
        ],
        1,
    ).astype(jnp.bfloat16)
    grad_joined = matmul_left(full_rows, grad_proj)
    grad_query_bias = jnp.sum(grad_proj[:, :head_cols], 0, dtype=jnp.float32)
    grad_value_bias = jnp.sum(grad_proj[:, 2 * head_cols :], 0, dtype=jnp.float32)
    grad_in = (
        lax.psum_scatter(
            matmul_right(grad_proj, joined).astype(jnp.bfloat16),
            "narrow",
            scatter_dimension=0,
            tiled=True,
        ).astype(jnp.float32)
        + grad_resid1
    ).astype(jnp.bfloat16)
    big_grads = (
        grad_joined[:, :head_cols],
        grad_query_bias,
        grad_joined[:, head_cols : 2 * head_cols],
        grad_joined[:, 2 * head_cols :],
        grad_value_bias,
        grad_out_weight,
        grad_inner_weight,
        grad_inner_bias,
        grad_outer_weight,
    )
    small_grads = (grad_out_bias, grad_gain1, grad_bias1, grad_outer_bias, grad_gain2, grad_bias2)
    return (result, grad_in, pooled, big_grads, small_grads)


def per_device(
    query_tokens,
    passage_tokens,
    query_cotangent,
    passage_cotangent,
    query_segments,
    passage_segments,
    query_cls,
    passage_cls,
    query_weight,
    query_bias,
    key_weight,
    value_weight,
    value_bias,
    out_weight,
    out_bias,
    norm1_gain,
    norm1_bias,
    inner_weight,
    inner_bias,
    outer_weight,
    outer_bias,
    norm2_gain,
    norm2_bias,
):
    weights = (
        query_weight,
        query_bias,
        key_weight,
        value_weight,
        value_bias,
        out_weight,
        out_bias,
        norm1_gain,
        norm1_bias,
        inner_weight,
        inner_bias,
        outer_weight,
        outer_bias,
        norm2_gain,
        norm2_bias,
    )
    passage = tower(passage_tokens, passage_cotangent, passage_segments, passage_cls, weights, 1)
    query = tower(query_tokens, query_cotangent, query_segments, query_cls, weights, 0)
    stacked = [
        jnp.stack([query_part, passage_part])
        for query_part, passage_part in zip(query[3], passage[3])
    ]
    layered = [
        jnp.stack([query_part, passage_part])
        for query_part, passage_part in zip(query[4], passage[4])
    ]
    big_grads = lax.psum(
        (
            stacked[0],
            stacked[1],
            stacked[2],
            stacked[3],
            stacked[4],
            stacked[5],
            stacked[6],
            stacked[7],
            stacked[8],
        ),
        "wide",
    )
    small_grads = lax.psum(
        (layered[0], layered[1], layered[2], layered[3], layered[4], layered[5]), ("wide", "narrow")
    )
    return (
        query[0],
        passage[0],
        query[1],
        passage[1],
        query[2],
        passage[2],
        big_grads[0],
        big_grads[1],
        big_grads[2],
        big_grads[3],
        big_grads[4],
        big_grads[5],
        small_grads[0],
        small_grads[1],
        small_grads[2],
        big_grads[6],
        big_grads[7],
        big_grads[8],
        small_grads[3],
        small_grads[4],
        small_grads[5],
    )


def solution(mesh):
    placed = (
        P(("wide", "narrow"), None),
        P(("wide", "narrow"), None),
        P(("wide", "narrow"), None),
        P(("wide", "narrow"), None),
        P("wide", None),
        P("wide", None),
        P("wide", None),
        P("wide", None),
        P(None, None, "narrow"),
        P(None, "narrow"),
        P(None, None, "narrow"),
        P(None, None, "narrow"),
        P(None, "narrow"),
        P(None, "narrow", None),
        P(),
        P(),
        P(),
        P(None, None, "narrow"),
        P(None, "narrow"),
        P(None, "narrow", None),
        P(),
        P(),
        P(),
    )
    return jax.shard_map(
        per_device,
        mesh=mesh,
        in_specs=placed,
        out_specs=(
            P(("wide", "narrow"), None),
            P(("wide", "narrow"), None),
            P(("wide", "narrow"), None),
            P(("wide", "narrow"), None),
            P("wide", None, "narrow"),
            P("wide", None, "narrow"),
            P(None, None, "narrow"),
            P(None, "narrow"),
            P(None, None, "narrow"),
            P(None, None, "narrow"),
            P(None, "narrow"),
            P(None, "narrow", None),
            P(),
            P(),
            P(),
            P(None, None, "narrow"),
            P(None, "narrow"),
            P(None, "narrow", None),
            P(),
            P(),
            P(),
        ),
        check_vma=False,
    )
```

profile of v0, /device:TPU:0, one launch (start us, length us, event | category | flops | bytes accessed | tf_op | source)
XLA Modules:
  0.0 994.1 jit_solution(7820239422888187306)
XLA Ops:
  12.2 50.1 %all-gather.5.cloned.1.call-done = bf16[1536,768]{1,0:T(8,128)(2,1)} async-done(((bf16[384,768]{1,0:T(8,128)(2,1)}), bf16[1536,768]{1,0:T(8,128)(2,1)}) %all-gather.5.cloned.1.call-update) | async-done | bytes 2359312 | tf_op jit(solution)/shard_map/all_gather | solution.py:119
  67.7 12.4 %while.4 = (s32[]{:T(128)}, bf16[3,512,3,64]{1,3,2,0:T(8,128)(2,1)S(1)}, f32[3,3,512,1]{2,1,3,0:T(4,128)}, bf16[3,512,3,64]{1,3,2,0:T(8,128)(2,1)S(1)}, s32[3,51...) while((s32[]{:T(128)}, ...), condition=%wide.region_11.12_spmd, body=%wide.region_8.11_spmd.sunk | while | flops 211290112 | bytes 11545701 | solution.py:127
  86.6 82.3 %reduce-scatter.19.cloned.1.call-done = f32[384,768]{1,0:T(8,128)} async-done(((f32[1536,768]{1,0:T(8,128)}), f32[384,768]{1,0:T(8,128)}) %reduce-scatter.19.cloned.1.call-update) | async-done | bytes 1179664 | tf_op jit(solution)/shard_map/reduce_scatter | solution.py:131
  173.4 49.8 %all-gather.7.cloned.1.call-done = bf16[1536,768]{1,0:T(8,128)(2,1)} async-done(((bf16[384,768]{1,0:T(8,128)(2,1)}), bf16[1536,768]{1,0:T(8,128)(2,1)}) %all-gather.7.cloned.1.call-update) | async-done | bytes 2359312 | tf_op jit(solution)/shard_map/all_gather | solution.py:137
  223.2 14.0 %fusion.49 = (bf16[1536,768]{1,0:T(8,128)(2,1)S(1)}, f32[1536,768]{1,0:T(8,128)}) fusion(f32[768]{0:T(1024)S(1)} %get-tuple-element.242, bf16[1536,768]{1,0:T(8,128)(2,1)} %all-gather.7.cloned.1.call-done, bf16[2,768,768]{2,1,0:T(8,128)(2,1)S(1)} %copy-done.103), kind=kOutput, calls=%fused_computation.64 | convolution fusion | flops 1889796096 | bytes 10620928 | tf_op jit(solution)/shard_map/dot_general | solution.py:13
  238.6 4.3 fusion.95
  243.8 27.2 %all_gather.24 = bf16[512,768]{1,0:T(8,128)(2,1)S(1)} all-gather(bf16[128,768]{1,0:T(8,128)(2,1)S(1)} %copy-done.43), channel_id=1, replica_groups=mesh['wide'=8,'narrow'=4] {'narrow'}, dimensions={0}, use_global_device_ids=true | all-gather | bytes 983040 | tf_op jit(solution)/shard_map/all_gather | solution.py:119
  279.2 57.7 %reduce-scatter.21.cloned.1.call-done = f32[384,768]{1,0:T(8,128)} async-done(((f32[1536,768]{1,0:T(8,128)}), f32[384,768]{1,0:T(8,128)}) %reduce-scatter.21.cloned.1.call-update) | async-done | bytes 1179664 | tf_op jit(solution)/shard_map/reduce_scatter | solution.py:140
  344.5 31.1 %reduce-scatter.15.cloned.1.call-done = f32[128,768]{1,0:T(8,128)} async-done(((f32[512,768]{1,0:T(8,128)}), f32[128,768]{1,0:T(8,128)}) %reduce-scatter.15.cloned.1.call-update) | async-done | bytes 393232 | tf_op jit(solution)/shard_map/reduce_scatter | solution.py:131
  377.9 24.8 %all_gather.25 = bf16[512,768]{1,0:T(8,128)(2,1)S(1)} all-gather(bf16[128,768]{1,0:T(8,128)(2,1)S(1)} %fusion.132), channel_id=1, replica_groups=mesh['wide'=8,'narrow'=4] {'narrow'}, dimensions={0}, use_global_device_ids=true | all-gather | bytes 983040 | tf_op jit(solution)/shard_map/all_gather | solution.py:137
  402.7 6.2 fusion.70
  411.8 21.3 %all-gather.9.cloned.1.call-done = bf16[1536,768]{1,0:T(8,128)(2,1)} async-done(((bf16[384,768]{1,0:T(8,128)(2,1)}), bf16[1536,768]{1,0:T(8,128)(2,1)}) %all-gather.9.cloned.1.call-update) | async-done | bytes 2359312 | tf_op jit(solution)/shard_map/all_gather | solution.py:157
  433.1 7.6 convert_reduce_fusion
  442.1 4.3 fusion.97
  446.4 23.7 %reduce-scatter.17.cloned.1.call-done = f32[128,768]{1,0:T(8,128)} async-done(((f32[512,768]{1,0:T(8,128)}), f32[128,768]{1,0:T(8,128)}) %reduce-scatter.17.cloned.1.call-update) | async-done | bytes 393232 | tf_op jit(solution)/shard_map/reduce_scatter | solution.py:140
  476.6 29.4 %all_gather.28 = bf16[512,768]{1,0:T(8,128)(2,1)S(1)} all-gather(bf16[128,768]{1,0:T(8,128)(2,1)S(1)} %convert_element_type.178), channel_id=1, replica_groups=mesh['wide'=8,'narrow'=4] {'narrow'}, dimensions={0}, use_global_device_ids=true | all-gather | bytes 983040 | tf_op jit(solution)/shard_map/all_gather | solution.py:157
  510.8 58.7 %reduce-scatter.27.cloned.1.call-done = f32[384,768]{1,0:T(8,128)} async-done(((f32[1536,768]{1,0:T(8,128)}), f32[384,768]{1,0:T(8,128)}) %reduce-scatter.27.cloned.1.call-update) | async-done | bytes 1179664 | tf_op jit(solution)/shard_map/reduce_scatter | solution.py:164
  581.0 27.0 %reduce-scatter.23.cloned.1.call-done = f32[128,768]{1,0:T(8,128)} async-done(((f32[512,768]{1,0:T(8,128)}), f32[128,768]{1,0:T(8,128)}) %reduce-scatter.23.cloned.1.call-update) | async-done | bytes 393232 | tf_op jit(solution)/shard_map/reduce_scatter | solution.py:164
  611.1 25.1 %all_gather.29 = bf16[512,768]{1,0:T(8,128)(2,1)S(1)} all-gather(bf16[128,768]{1,0:T(8,128)(2,1)S(1)} %convert_element_type.180), channel_id=1, replica_groups=mesh['wide'=8,'narrow'=4] {'narrow'}, dimensions={0}, use_global_device_ids=true | all-gather | bytes 983040 | tf_op jit(solution)/shard_map/all_gather | solution.py:173
  646.6 19.5 %all-gather.11.cloned.1.call-done = bf16[1536,768]{1,0:T(8,128)(2,1)} async-done(((bf16[384,768]{1,0:T(8,128)(2,1)}), bf16[1536,768]{1,0:T(8,128)(2,1)}) %all-gather.11.cloned.1.call-update) | async-done | bytes 2359312 | tf_op jit(solution)/shard_map/all_gather | solution.py:173
  670.3 20.4 %while.5 = (s32[]{:T(128)}, bf16[3,512,3,64]{1,3,2,0:T(8,128)(2,1)S(1)}, bf16[3,512,3,64]{1,3,2,0:T(8,128)(2,1)S(1)}, bf16[3,512,3,64]{1,3,2,0:T(8,128)(2,1)S(1)...) while((s32[]{:T(128)}, ...), condition=%wide.region_32.33_spmd, body=%wide.region_30.32_spmd.sunk | while | flops 511114240 | bytes 26718332 | solution.py:176
  734.1 43.5 %all-reduce = (f32[2,768]{1,0:T(2,128)}, f32[2,768]{1,0:T(2,128)}, f32[2,768]{1,0:T(2,128)}, f32[2,768]{1,0:T(2,128)}, f32[2,768]{1,0:T(2,128)}, /*index=5*/f32[2,768]{1,0:T(2,128)}) all-reduce(f32[2,768]{1,0:T(2,128)S(1)} %pad_maximum_fusion.15, ...), channel_id=1, replica_groups=mesh['wide'=8,'narrow'=4] {'wide','narrow'}, use_global_device_ids=true, to_apply=%region_48.49 | all-reduce | flops 9216 | bytes 73728 | tf_op jit(solution)/shard_map/psum | solution.py:281
  778.0 23.7 %all-reduce.1 = (f32[2,192]{1,0:T(2,128)}, f32[2,192]{1,0:T(2,128)}, f32[2,768]{1,0:T(2,128)}) all-reduce(f32[2,192]{1,0:T(2,128)S(1)} %pad_maximum_fusion.22, f32[2,192]{1,0:T(2,128)S(1)} %pad_maximum_fusion.23, f32[2,768]{1,0:T(2,128)S(1)} %pad_maximum_fusion.18), channel_id=1, replica_groups=mesh['wide'=8,'narrow'=4] {'wide'}, use_global_device_ids=true, to_apply=%region_39.40 | all-reduce | flops 2304 | bytes 18432 | tf_op jit(solution)/shard_map/psum | solution.py:267
  803.7 172.8 %all-reduce.5.cloned.1.call-done = (f32[2,768,192]{1,2,0:T(8,128)}, f32[2,768,192]{1,2,0:T(8,128)}, f32[2,768,192]{1,2,0:T(8,128)}, f32[2,192,768]{2,1,0:T(8,128...) async-done(((f32[2,768,192]{1,2,0:T(8,128)}, f32[2,768,192]{1,2,0:T(8,128)}, f32[2,768,192]{1,2,0:T(8,128)}, f32[2,192,768]{2,1,0:T(8,128)}, f32[2,768,768]{2,1,0:T(8,128)}, ...) | async-done | bytes 14155792 | tf_op jit(solution)/shard_map/psum | solution.py:267
  (479 shorter events, 174.2 us)
Async XLA Ops:
  7.2 55.1 %all-gather.5.cloned.1.call-start = ((), (), s32[]{:S(2)}) async-start(), calls=%async_computation.12 | async-start | bytes 2949120 | tf_op jit(solution)/shard_map/all_gather | solution.py:119
  7.9 161.0 %reduce-scatter.19.cloned.1.call-start = ((), (), s32[]{:S(2)}) async-start(), calls=%async_computation.13 | async-start | bytes 5898240 | tf_op jit(solution)/shard_map/reduce_scatter | solution.py:131
  11.4 51.0 %copy-start.64 = (bf16[768,192]{0,1:T(8,128)(2,1)}, bf16[768,192]{0,1:T(8,128)(2,1)S(1)}, u32[]{:S(2)}) copy-start(bf16[768,192]{0,1:T(8,128)(2,1)S(1)} %get-tuple-element.336) | copy-start | bytes 884740
  12.2 53.4 %copy-start.56 = (bf16[768,192]{0,1:T(8,128)(2,1)}, bf16[768,192]{0,1:T(8,128)(2,1)S(1)}, u32[]{:S(2)}) copy-start(bf16[768,192]{0,1:T(8,128)(2,1)S(1)} %get-tuple-element.340) | copy-start | bytes 884740
  12.2 53.4 %copy-start.58 = (bf16[768,192]{0,1:T(8,128)(2,1)}, bf16[768,192]{0,1:T(8,128)(2,1)S(1)}, u32[]{:S(2)}) copy-start(bf16[768,192]{0,1:T(8,128)(2,1)S(1)} %get-tuple-element.362) | copy-start | bytes 884740
  12.2 258.9 %copy-start.60 = (bf16[768,192]{0,1:T(8,128)(2,1)}, bf16[768,192]{0,1:T(8,128)(2,1)S(1)}, u32[]{:S(2)}) copy-start(bf16[768,192]{0,1:T(8,128)(2,1)S(1)} %get-tuple-element.341) | copy-start | bytes 884740
  84.7 84.2 %copy-start.26 = (bf16[384,768]{1,0:T(8,128)(2,1)S(1)}, bf16[384,768]{1,0:T(8,128)(2,1)}, u32[]{:S(2)}) copy-start(bf16[384,768]{1,0:T(8,128)(2,1)} %param.28) | copy-start | bytes 1769476
  84.7 138.5 %all-gather.7.cloned.1.call-start = ((), (), s32[]{:S(2)}) async-start(), calls=%async_computation.14 | async-start | bytes 2949120 | tf_op jit(solution)/shard_map/all_gather | solution.py:137
  170.4 52.7 %copy-start.103 = (bf16[2,768,768]{2,1,0:T(8,128)(2,1)S(1)}, bf16[2,768,768]{2,1,0:T(8,128)(2,1)}, u32[]{:S(2)}) copy-start(bf16[2,768,768]{2,1,0:T(8,128)(2,1)} %param.44) | copy-start | bytes 7077892
  172.5 164.5 %reduce-scatter.21.cloned.1.call-start = ((), (), s32[]{:S(2)}) async-start(), calls=%async_computation.15 | async-start | bytes 5898240 | tf_op jit(solution)/shard_map/reduce_scatter | solution.py:140
  173.4 63.8 %copy-start.95 = (f32[768]{0:T(1024)}, f32[768]{0:T(1024)S(1)}, u32[]{:S(2)}) copy-start(f32[768]{0:T(1024)S(1)} %get-tuple-element.242) | copy-start | bytes 9220
  242.9 132.6 %reduce-scatter.15.cloned.1.call-start = ((), (), s32[]{:S(2)}) async-start(), calls=%async_computation.10 | async-start | bytes 1966080 | tf_op jit(solution)/shard_map/reduce_scatter | solution.py:131
  277.9 155.2 %all-gather.9.cloned.1.call-start = ((), (), s32[]{:S(2)}) async-start(), calls=%async_computation.18 | async-start | bytes 2949120 | tf_op jit(solution)/shard_map/all_gather | solution.py:157
  344.4 125.8 %reduce-scatter.17.cloned.1.call-start = ((), (), s32[]{:S(2)}) async-start(), calls=%async_computation.11 | async-start | bytes 1966080 | tf_op jit(solution)/shard_map/reduce_scatter | solution.py:140
  411.8 157.6 %reduce-scatter.27.cloned.1.call-start = ((), (), s32[]{:S(2)}) async-start(), calls=%async_computation.19 | async-start | bytes 5898240 | tf_op jit(solution)/shard_map/reduce_scatter | solution.py:164
  446.4 161.5 %reduce-scatter.23.cloned.1.call-start = ((), (), s32[]{:S(2)}) async-start(), calls=%async_computation.16 | async-start | bytes 1966080 | tf_op jit(solution)/shard_map/reduce_scatter | solution.py:164
  470.2 35.9 %copy-start.113 = (f32[512,768]{1,0:T(8,128)S(1)}, f32[512,768]{1,0:T(8,128)}, u32[]{:S(2)}) copy-start(f32[512,768]{1,0:T(8,128)} %get-tuple-element.352) | copy-start | bytes 4718596
  510.7 155.4 %all-gather.11.cloned.1.call-start = ((), (), s32[]{:S(2)}) async-start(), calls=%async_computation.20 | async-start | bytes 2949120 | tf_op jit(solution)/shard_map/all_gather | solution.py:173
  575.7 149.0 %reduce-scatter.31.cloned.1.call-start = ((), (), s32[]{:S(2)}) async-start(), calls=%async_computation.22 | async-start | bytes 245760
  580.9 145.6 %reduce-scatter.25.cloned.1.call-start = ((), (), s32[]{:S(2)}) async-start(), calls=%async_computation.17 | async-start | bytes 983040 | tf_op jit(solution)/shard_map/reduce_scatter | solution.py:192
  644.4 87.9 %reduce-scatter.33.cloned.1.call-start = ((), (), s32[]{:S(2)}) async-start(), calls=%async_computation.23 | async-start | bytes 245760
  646.5 155.1 %reduce-scatter.29.cloned.1.call-start = ((), (), s32[]{:S(2)}) async-start(), calls=%async_computation.21 | async-start | bytes 2949120 | tf_op jit(solution)/shard_map/reduce_scatter | solution.py:192
  698.0 278.5 %all-reduce.5.cloned.1.call-start = ((), (), s32[]{:S(2)}) async-start(), calls=%async_computation.24 | async-start | bytes 28311552 | tf_op jit(solution)/shard_map/psum | solution.py:267
  724.0 77.7 %copy-start.7 = (f32[384,768]{1,0:T(8,128)S(1)}, f32[384,768]{1,0:T(8,128)}, u32[]{:S(2)}) copy-start(f32[384,768]{1,0:T(8,128)} %copy-done.6) | copy-start | bytes 3538948
  (107 other events, 557.3 us)
Sparse Core Ops, SparseCore 0:
  9.6 52.6 all-gather.4
  84.8 84.0 reduce-scatter.18
  172.6 50.4 all-gather.6
  243.1 93.8 reduce-scatter.20
  339.1 36.3 reduce-scatter.14
  377.5 55.5 all-gather.8
  435.4 34.6 reduce-scatter.16
  473.0 96.3 reduce-scatter.26
  571.7 36.1 reduce-scatter.22
  609.9 56.0 all-gather.10
  668.3 18.8 reduce-scatter.30
  689.4 21.4 reduce-scatter.24
  713.1 19.1 reduce-scatter.32
  734.4 46.9 reduce-scatter.28
  787.7 188.7 all-reduce.4
where the time goes:
time: 1000 us; the launch traced here: 994 us
  waiting for transfers between devices  599 us (60%)
  blocking collectives  174 us (17%)
  matrix products  92.8 us (9%)
  local copies, waits for them, and re-layouts  58 us (6%)
  other arithmetic  53.8 us (5%)
  between operations  15.6 us (2%)
    psum x1, waiting for transfers between devices, per_device(): lax.psum((stacked[0], stacked[1], stacked[2], stacked[3], stacked[4], sta...  173 us
    reduce_scatter x2, waiting for transfers between devices, tower(): lax.psum_scatter(matmul(attended, out_weight), 'narrow', scatter_dimensio...  113 us
    reduce_scatter x2, waiting for transfers between devices, tower(): lax.psum_scatter(matmul_right(grad_inner, inner_weight), 'narrow', scatte...  85.6 us
    reduce_scatter x2, waiting for transfers between devices, tower(): lax.psum_scatter(matmul(activated, outer_weight), 'narrow', scatter_dimen...  81.5 us
    all_gather x1, waiting for transfers between devices, tower(): full_rows = lax.all_gather(tokens, 'narrow', axis=0, tiled=True)  50.1 us
    all_gather x1, waiting for transfers between devices, tower(): lax.all_gather(hidden1.astype(jnp.bfloat16), 'narrow', axis=0, tiled=True)  49.8 us
    unnamed x252, local copies, waits for them, and re-layouts  43.6 us
    psum x1, blocking collectives, per_device(): lax.psum((layered[0], layered[1], layered[2], layered[3], layered[4], lay...  43.5 us
  transfers between devices with their start and end apart: 15, of which 12 were waited for; matrix products, arithmetic and copies ran while one was open for 13% of the time, Pallas kernels for 0%

commit v1 on v0

--- a/solution.py
+++ b/solution.py
@@ -7,6 +7,27 @@
 HDIM = 64
 NORM_EPS = 1e-05
 MASKED = -1e30
+
+
+def gather_around(x, axis, dim):
+    count, mine, rows = (lax.axis_size(axis), lax.axis_index(axis), x.shape[dim])
+    ahead = [(i, (i + 1) % count) for i in range(count)]
+    left = [(i, (i - 1) % count) for i in range(count)]
+    out = jnp.zeros((*x.shape[:dim], count * rows, *x.shape[dim + 1 :]), x.dtype)
+    out = lax.dynamic_update_slice_in_dim(out, x, mine * rows, axis=dim)
+    from_left = from_right = x
+    middle = count // 2
+    for turn in range(1, middle + 1):
+        from_left = lax.ppermute(from_left, axis, ahead)
+        out = lax.dynamic_update_slice_in_dim(
+            out, from_left, (mine - turn) % count * rows, axis=dim
+        )
+        if turn < count - middle:
+            from_right = lax.ppermute(from_right, axis, left)
+            out = lax.dynamic_update_slice_in_dim(
+                out, from_right, (mine + turn) % count * rows, axis=dim
+            )
+    return out
 
 
 def matmul(left, right):
@@ -170,7 +191,7 @@
     grad_bias1 = jnp.sum(grad_hidden1, 0)
     grad_resid1 = norm_back(grad_hidden1, normed1, inverse1, norm1_gain)
     grad_out_bias = jnp.sum(grad_resid1, 0)
-    resid1_full = lax.all_gather(grad_resid1.astype(jnp.bfloat16), "narrow", axis=0, tiled=True)
+    resid1_full = gather_around(grad_resid1.astype(jnp.bfloat16), "narrow", 0)
     grad_out_weight = matmul_left(attended, resid1_full)
     grad_attended = matmul_right(resid1_full, out_weight).astype(jnp.bfloat16).reshape(split_shape)
     grad_query, grad_key, grad_value = lax.map(

time: 1000 us -> 966 us (0.966)
  waiting for transfers between devices: 599 us -> 557 us
  blocking collectives: 174 us -> 146 us
  local copies, waits for them, and re-layouts: 58 us -> 75.4 us
  starting transfers between devices: 1.01 us -> 11.7 us
    ppermute x0 -> x6, waiting for transfers between devices: none -> 54.4 us  [the longest x4 44.7 us: gather_around(): from_left = lax.ppermute(from_left, axis, ahead)]
    psum x1, waiting for transfers between devices: 173 us -> 142 us  [per_device(): lax.psum((stacked[0], stacked[1], stacked[2], stacked[3], stacked[4], sta...]
    all_gather x1, waiting for transfers between devices: 49.8 us -> 24.2 us  [tower(): lax.all_gather(hidden1.astype(jnp.bfloat16), 'narrow', axis=0, tiled=True)]
    all_gather x1 -> x0, blocking collectives: 25.1 us -> none  [tower(): lax.all_gather(grad_resid1.astype(jnp.bfloat16), 'narrow', axis=0, tiled=...]
    all_gather x1 -> x0, waiting for transfers between devices: 19.5 us -> none  [tower(): lax.all_gather(grad_resid1.astype(jnp.bfloat16), 'narrow', axis=0, tiled=...]
    reduce_scatter x2, waiting for transfers between devices: 113 us -> 99.5 us  [tower(): lax.psum_scatter(matmul(attended, out_weight), 'narrow', scatter_dimensio...]
    ppermute x0 -> x6, starting transfers between devices: none -> 10.4 us  [the longest x2 5.78 us: gather_around(): from_right = lax.ppermute(from_right, axis, left)]
    unnamed x252 -> x248, local copies, waits for them, and re-layouts: 43.6 us -> 37.9 us
  transfers between devices with their start and end apart: 15 -> 20, of which waited for: 12 -> 16; matrix products, arithmetic and copies ran while one was open for 13% -> 17% of each run, Pallas kernels for 0% -> 0%
where the time goes in v1:
time: 966 us; the launch traced here: 956 us
  waiting for transfers between devices  557 us (58%)
  blocking collectives  146 us (15%)
  matrix products  95.9 us (10%)
  local copies, waits for them, and re-layouts  75.4 us (8%)
  other arithmetic  54.2 us (6%)
  between operations  15.6 us (2%)
  starting transfers between devices  11.7 us (1%)
    psum x1, waiting for transfers between devices, per_device(): lax.psum((stacked[0], stacked[1], stacked[2], stacked[3], stacked[4], sta...  142 us
    reduce_scatter x2, waiting for transfers between devices, tower(): lax.psum_scatter(matmul(attended, out_weight), 'narrow', scatter_dimensio...  99.5 us
    reduce_scatter x2, waiting for transfers between devices, tower(): lax.psum_scatter(matmul(activated, outer_weight), 'narrow', scatter_dimen...  86.4 us
    reduce_scatter x2, waiting for transfers between devices, tower(): lax.psum_scatter(matmul_right(grad_inner, inner_weight), 'narrow', scatte...  77.6 us
    all_gather x1, waiting for transfers between devices, tower(): full_rows = lax.all_gather(tokens, 'narrow', axis=0, tiled=True)  50.2 us
    ppermute x4, waiting for transfers between devices, gather_around(): from_left = lax.ppermute(from_left, axis, ahead)  44.7 us
    psum x1, blocking collectives, per_device(): lax.psum((layered[0], layered[1], layered[2], layered[3], layered[4], lay...  43.3 us
    unnamed x248, local copies, waits for them, and re-layouts  37.9 us
  transfers between devices with their start and end apart: 20, of which 16 were waited for; matrix products, arithmetic and copies ran while one was open for 17% of the time, Pallas kernels for 0%

profile of v1, /device:TPU:0, one launch (start us, length us, event | category | flops | bytes accessed | tf_op | source)
XLA Modules:
  0.0 956.2 jit_solution(4858402782248060281)
XLA Ops:
  12.2 50.2 %all-gather.4.cloned.1.call-done = bf16[1536,768]{1,0:T(8,128)(2,1)} async-done(((bf16[384,768]{1,0:T(8,128)(2,1)}), bf16[1536,768]{1,0:T(8,128)(2,1)}) %all-gather.4.cloned.1.call-update) | async-done | bytes 2359312 | tf_op jit(solution)/shard_map/all_gather | solution.py:140
  67.7 12.4 %while.4 = (s32[]{:T(128)}, bf16[3,512,3,64]{1,3,2,0:T(8,128)(2,1)S(1)}, f32[3,3,512,1]{2,1,3,0:T(4,128)}, bf16[3,512,3,64]{1,3,2,0:T(8,128)(2,1)S(1)}, s32[3,51...) while((s32[]{:T(128)}, ...), condition=%wide.region_11.12_spmd, body=%wide.region_8.11_spmd.sunk | while | flops 211290112 | bytes 11545701 | solution.py:148
  86.6 82.3 %reduce-scatter.19.cloned.1.call-done = f32[384,768]{1,0:T(8,128)} async-done(((f32[1536,768]{1,0:T(8,128)}), f32[384,768]{1,0:T(8,128)}) %reduce-scatter.19.cloned.1.call-update) | async-done | bytes 1179664 | tf_op jit(solution)/shard_map/reduce_scatter | solution.py:152
  172.6 24.0 %all_gather.18 = bf16[512,768]{1,0:T(8,128)(2,1)S(1)} all-gather(bf16[128,768]{1,0:T(8,128)(2,1)S(1)} %copy-done.48), channel_id=1, replica_groups=mesh['wide'=8,'narrow'=4] {'narrow'}, dimensions={0}, use_global_device_ids=true | all-gather | bytes 983040 | tf_op jit(solution)/shard_map/all_gather | solution.py:140
  204.3 24.2 %all-gather.6.cloned.1.call-done = bf16[1536,768]{1,0:T(8,128)(2,1)} async-done(((bf16[384,768]{1,0:T(8,128)(2,1)}), bf16[1536,768]{1,0:T(8,128)(2,1)}) %all-gather.6.cloned.1.call-update) | async-done | bytes 2359312 | tf_op jit(solution)/shard_map/all_gather | solution.py:158
  228.5 14.4 %fusion.49 = (bf16[1536,768]{1,0:T(8,128)(2,1)S(1)}, f32[1536,768]{1,0:T(8,128)}) fusion(f32[768]{0:T(1024)S(1)} %get-tuple-element.242, bf16[1536,768]{1,0:T(8,128)(2,1)} %all-gather.6.cloned.1.call-done, bf16[2,768,768]{2,1,0:T(8,128)(2,1)} %param.44), kind=kOutput, calls=%fused_computation.64 | convolution fusion | flops 1889796096 | bytes 10619904 | tf_op jit(solution)/shard_map/dot_general | solution.py:34
  248.7 17.2 %reduce-scatter.15.cloned.1.call-done = f32[128,768]{1,0:T(8,128)} async-done(((f32[512,768]{1,0:T(8,128)}), f32[128,768]{1,0:T(8,128)}) %reduce-scatter.15.cloned.1.call-update) | async-done | bytes 393232 | tf_op jit(solution)/shard_map/reduce_scatter | solution.py:152
  268.3 25.8 %all_gather.19 = bf16[512,768]{1,0:T(8,128)(2,1)S(1)} all-gather(bf16[128,768]{1,0:T(8,128)(2,1)S(1)} %fusion.132), channel_id=1, replica_groups=mesh['wide'=8,'narrow'=4] {'narrow'}, dimensions={0}, use_global_device_ids=true | all-gather | bytes 983040 | tf_op jit(solution)/shard_map/all_gather | solution.py:158
  305.9 55.5 %reduce-scatter.21.cloned.1.call-done = f32[384,768]{1,0:T(8,128)} async-done(((f32[1536,768]{1,0:T(8,128)}), f32[384,768]{1,0:T(8,128)}) %reduce-scatter.21.cloned.1.call-update) | async-done | bytes 1179664 | tf_op jit(solution)/shard_map/reduce_scatter | solution.py:161
  368.9 31.0 %reduce-scatter.17.cloned.1.call-done = f32[128,768]{1,0:T(8,128)} async-done(((f32[512,768]{1,0:T(8,128)}), f32[128,768]{1,0:T(8,128)}) %reduce-scatter.17.cloned.1.call-update) | async-done | bytes 393232 | tf_op jit(solution)/shard_map/reduce_scatter | solution.py:161
  406.4 28.5 %all_gather.22 = bf16[512,768]{1,0:T(8,128)(2,1)S(1)} all-gather(bf16[128,768]{1,0:T(8,128)(2,1)S(1)} %convert_element_type.178), channel_id=1, replica_groups=mesh['wide'=8,'narrow'=4] {'narrow'}, dimensions={0}, use_global_device_ids=true | all-gather | bytes 983040 | tf_op jit(solution)/shard_map/all_gather | solution.py:178
  439.6 21.4 %all-gather.8.cloned.1.call-done = bf16[1536,768]{1,0:T(8,128)(2,1)} async-done(((bf16[384,768]{1,0:T(8,128)(2,1)}), bf16[1536,768]{1,0:T(8,128)(2,1)}) %all-gather.8.cloned.1.call-update) | async-done | bytes 2359312 | tf_op jit(solution)/shard_map/all_gather | solution.py:178
  461.0 7.6 convert_reduce_fusion
  474.4 24.1 %reduce-scatter.23.cloned.1.call-done = f32[128,768]{1,0:T(8,128)} async-done(((f32[512,768]{1,0:T(8,128)}), f32[128,768]{1,0:T(8,128)}) %reduce-scatter.23.cloned.1.call-update) | async-done | bytes 393232 | tf_op jit(solution)/shard_map/reduce_scatter | solution.py:185
  511.1 7.0 collective-permute-done
  525.6 7.8 collective-permute-done.2
  543.0 53.6 %reduce-scatter.27.cloned.1.call-done = f32[384,768]{1,0:T(8,128)} async-done(((f32[1536,768]{1,0:T(8,128)}), f32[384,768]{1,0:T(8,128)}) %reduce-scatter.27.cloned.1.call-update) | async-done | bytes 1179664 | tf_op jit(solution)/shard_map/reduce_scatter | solution.py:185
  606.1 17.1 %collective-permute-done.3 = bf16[384,768]{1,0:T(8,128)(2,1)} collective-permute-done((bf16[384,768]{1,0:T(8,128)(2,1)S(1)}, bf16[384,768]{1,0:T(8,128)(2,1)}, u32[]{:S(2)}, u32[]{:S(2)}) %collective-permute-start.3) | collective-permute-done | bytes 589856 | tf_op jit(solution)/shard_map/ppermute | solution.py:21
  627.2 8.1 collective-permute-done.4
  637.2 12.9 %collective-permute-done.5 = bf16[384,768]{1,0:T(8,128)(2,1)} collective-permute-done((bf16[384,768]{1,0:T(8,128)(2,1)}, bf16[384,768]{1,0:T(8,128)(2,1)}, u32[]{:S(2)}, u32[]{:S(2)}) %collective-permute-start.5) | collective-permute-done | bytes 589856 | tf_op jit(solution)/shard_map/ppermute | solution.py:21
  659.1 26.9 %while.5 = (s32[]{:T(128)}, bf16[3,512,3,64]{1,3,2,0:T(8,128)(2,1)}, bf16[3,512,3,64]{1,3,2,0:T(8,128)(2,1)}, bf16[3,512,3,64]{1,3,2,0:T(8,128)(2,1)S(1)}, bf16[...) while((s32[]{:T(128)}, ...), condition=%wide.region_32.33_spmd, body=%wide.region_30.32_spmd.sunk | while | flops 511114240 | bytes 36155628 | solution.py:197
  726.2 43.3 %all-reduce = (f32[2,768]{1,0:T(2,128)}, f32[2,768]{1,0:T(2,128)}, f32[2,768]{1,0:T(2,128)}, f32[2,768]{1,0:T(2,128)}, f32[2,768]{1,0:T(2,128)}, /*index=5*/f32[2,768]{1,0:T(2,128)}) all-reduce(f32[2,768]{1,0:T(2,128)S(1)} %pad_maximum_fusion.15, ...), channel_id=1, replica_groups=mesh['wide'=8,'narrow'=4] {'wide','narrow'}, use_global_device_ids=true, to_apply=%region_48.49 | all-reduce | flops 9216 | bytes 73728 | tf_op jit(solution)/shard_map/psum | solution.py:302
  769.8 24.8 %all-reduce.1 = (f32[2,192]{1,0:T(2,128)}, f32[2,192]{1,0:T(2,128)}, f32[2,768]{1,0:T(2,128)}) all-reduce(f32[2,192]{1,0:T(2,128)S(1)} %pad_maximum_fusion.22, f32[2,192]{1,0:T(2,128)S(1)} %pad_maximum_fusion.23, f32[2,768]{1,0:T(2,128)S(1)} %pad_maximum_fusion.18), channel_id=1, replica_groups=mesh['wide'=8,'narrow'=4] {'wide'}, use_global_device_ids=true, to_apply=%region_39.40 | all-reduce | flops 2304 | bytes 18432 | tf_op jit(solution)/shard_map/psum | solution.py:288
  796.7 142.0 %all-reduce.5.cloned.1.call-done = (f32[2,768,192]{1,2,0:T(8,128)}, f32[2,768,192]{1,2,0:T(8,128)}, f32[2,768,192]{1,2,0:T(8,128)}, f32[2,192,768]{2,1,0:T(8,128...) async-done(((f32[2,768,192]{1,2,0:T(8,128)}, f32[2,768,192]{1,2,0:T(8,128)}, f32[2,768,192]{1,2,0:T(8,128)}, f32[2,192,768]{2,1,0:T(8,128)}, f32[2,768,768]{2,1,0:T(8,128)}, ...) | async-done | bytes 14155792 | tf_op jit(solution)/shard_map/psum | solution.py:288
  (515 shorter events, 217.7 us)
Async XLA Ops:
  7.2 55.1 %all-gather.4.cloned.1.call-start = ((), (), s32[]{:S(2)}) async-start(), calls=%async_computation.12 | async-start | bytes 2949120 | tf_op jit(solution)/shard_map/all_gather | solution.py:140
  7.9 160.9 %reduce-scatter.19.cloned.1.call-start = ((), (), s32[]{:S(2)}) async-start(), calls=%async_computation.13 | async-start | bytes 5898240 | tf_op jit(solution)/shard_map/reduce_scatter | solution.py:152
  12.2 184.4 %copy-start.64 = (bf16[768,192]{0,1:T(8,128)(2,1)}, bf16[768,192]{0,1:T(8,128)(2,1)S(1)}, u32[]{:S(2)}) copy-start(bf16[768,192]{0,1:T(8,128)(2,1)S(1)} %get-tuple-element.345) | copy-start | bytes 884740
  84.7 84.2 %copy-start.25 = (bf16[384,768]{1,0:T(8,128)(2,1)S(1)}, bf16[384,768]{1,0:T(8,128)(2,1)}, u32[]{:S(2)}) copy-start(bf16[384,768]{1,0:T(8,128)(2,1)} %param.28) | copy-start | bytes 1769476
  84.7 143.8 %all-gather.6.cloned.1.call-start = ((), (), s32[]{:S(2)}) async-start(), calls=%async_computation.14 | async-start | bytes 2949120 | tf_op jit(solution)/shard_map/all_gather | solution.py:158
  86.6 84.2 %copy-start.79 = (f32[768]{0:T(1024)}, f32[768]{0:T(1024)S(1)}, u32[]{:S(2)}) copy-start(f32[768]{0:T(1024)S(1)} %get-tuple-element.246) | copy-start | bytes 9220
  172.5 93.4 %reduce-scatter.15.cloned.1.call-start = ((), (), s32[]{:S(2)}) async-start(), calls=%async_computation.10 | async-start | bytes 1966080 | tf_op jit(solution)/shard_map/reduce_scatter | solution.py:152
  203.5 157.9 %reduce-scatter.21.cloned.1.call-start = ((), (), s32[]{:S(2)}) async-start(), calls=%async_computation.15 | async-start | bytes 5898240 | tf_op jit(solution)/shard_map/reduce_scatter | solution.py:161
  248.6 151.3 %reduce-scatter.17.cloned.1.call-start = ((), (), s32[]{:S(2)}) async-start(), calls=%async_computation.11 | async-start | bytes 1966080 | tf_op jit(solution)/shard_map/reduce_scatter | solution.py:161
  303.1 157.9 %all-gather.8.cloned.1.call-start = ((), (), s32[]{:S(2)}) async-start(), calls=%async_computation.18 | async-start | bytes 2949120 | tf_op jit(solution)/shard_map/all_gather | solution.py:178
  368.9 129.5 %reduce-scatter.23.cloned.1.call-start = ((), (), s32[]{:S(2)}) async-start(), calls=%async_computation.16 | async-start | bytes 1966080 | tf_op jit(solution)/shard_map/reduce_scatter | solution.py:185
  439.5 157.1 %reduce-scatter.27.cloned.1.call-start = ((), (), s32[]{:S(2)}) async-start(), calls=%async_computation.19 | async-start | bytes 5898240 | tf_op jit(solution)/shard_map/reduce_scatter | solution.py:185
  474.2 246.5 %reduce-scatter.31.cloned.1.call-start = ((), (), s32[]{:S(2)}) async-start(), calls=%async_computation.21 | async-start | bytes 245760
  504.2 13.9 %collective-permute-start = (bf16[128,768]{1,0:T(8,128)(2,1)}, bf16[128,768]{1,0:T(8,128)(2,1)}, u32[]{:S(2)}, u32[]{:S(2)}) collective-permute-start(bf16[128,768]{1,0:T(8,128)(2,1)} %get-tuple-element.315), channel_id=1, source_target_pairs={{0,1},{1,2},{2,3},{3,0},{4,5},{5,6},{6,7},{7,4},{8,9},{9,10},{10,1... | collective-permute-start | bytes 589832 | tf_op jit(solution)/shard_map/ppermute | solution.py:21
  504.4 19.6 %collective-permute-start.1 = (bf16[128,768]{1,0:T(8,128)(2,1)}, bf16[128,768]{1,0:T(8,128)(2,1)}, u32[]{:S(2)}, u32[]{:S(2)}) collective-permute-start(bf16[128,768]{1,0:T(8,128)(2,1)} %get-tuple-element.315), channel_id=1, source_target_pairs={{0,3},{1,0},{2,1},{3,2},{4,7},{5,4},{6,5},{7,6},{8,11},{9,8},{10,9... | collective-permute-start | bytes 589832 | tf_op jit(solution)/shard_map/ppermute | solution.py:26
  511.1 211.5 %reduce-scatter.25.cloned.1.call-start = ((), (), s32[]{:S(2)}) async-start(), calls=%async_computation.17 | async-start | bytes 983040 | tf_op jit(solution)/shard_map/reduce_scatter | solution.py:213
  518.1 15.3 %collective-permute-start.2 = (bf16[128,768]{1,0:T(8,128)(2,1)}, bf16[128,768]{1,0:T(8,128)(2,1)S(1)}, u32[]{:S(2)}, u32[]{:S(2)}) collective-permute-start(bf16[128,768]{1,0:T(8,128)(2,1)} %collective-permute-done), channel_id=1, source_target_pairs={{0,1},{1,2},{2,3},{3,0},{4,5},{5,6},{6,7},{7,4},{8,9},{9,10},{10,1... | collective-permute-start | bytes 589832 | tf_op jit(solution)/shard_map/ppermute | solution.py:21
  540.8 55.8 %copy-start.1 = (f32[384,768]{1,0:T(8,128)S(1)}, f32[384,768]{1,0:T(8,128)}, u32[]{:S(2)}) copy-start(f32[384,768]{1,0:T(8,128)} %copy-done) | copy-start | bytes 3538948
  542.6 181.8 %reduce-scatter.33.cloned.1.call-start = ((), (), s32[]{:S(2)}) async-start(), calls=%async_computation.22 | async-start | bytes 245760
  602.1 21.1 %collective-permute-start.3 = (bf16[384,768]{1,0:T(8,128)(2,1)S(1)}, bf16[384,768]{1,0:T(8,128)(2,1)}, u32[]{:S(2)}, u32[]{:S(2)}) collective-permute-start(bf16[384,768]{1,0:T(8,128)(2,1)S(1)} %get-tuple-element.312), channel_id=1, source_target_pairs={{0,1},{1,2},{2,3},{3,0},{4,5},{5,6},{6,7},{7,4},{8,9},{9,10},{10,1... | collective-permute-start | bytes 1769480 | tf_op jit(solution)/shard_map/ppermute | solution.py:21
  603.8 31.5 %collective-permute-start.4 = (bf16[384,768]{1,0:T(8,128)(2,1)S(1)}, bf16[384,768]{1,0:T(8,128)(2,1)}, u32[]{:S(2)}, u32[]{:S(2)}) collective-permute-start(bf16[384,768]{1,0:T(8,128)(2,1)S(1)} %get-tuple-element.312), channel_id=1, source_target_pairs={{0,3},{1,0},{2,1},{3,2},{4,7},{5,4},{6,5},{7,6},{8,11},{9,8},{10,9... | collective-permute-start | bytes 1769480 | tf_op jit(solution)/shard_map/ppermute | solution.py:26
  623.2 26.9 %collective-permute-start.5 = (bf16[384,768]{1,0:T(8,128)(2,1)}, bf16[384,768]{1,0:T(8,128)(2,1)}, u32[]{:S(2)}, u32[]{:S(2)}) collective-permute-start(bf16[384,768]{1,0:T(8,128)(2,1)} %collective-permute-done.3), channel_id=1, source_target_pairs={{0,1},{1,2},{2,3},{3,0},{4,5},{5,6},{6,7},{7,4},{8,9},{9,10},{10,1... | collective-permute-start | bytes 1769480 | tf_op jit(solution)/shard_map/ppermute | solution.py:21
  625.2 169.5 %reduce-scatter.29.cloned.1.call-start = ((), (), s32[]{:S(2)}) async-start(), calls=%async_computation.20 | async-start | bytes 2949120 | tf_op jit(solution)/shard_map/reduce_scatter | solution.py:213
  693.3 245.3 %all-reduce.5.cloned.1.call-start = ((), (), s32[]{:S(2)}) async-start(), calls=%async_computation.23 | async-start | bytes 28311552 | tf_op jit(solution)/shard_map/psum | solution.py:288
  (122 other events, 813.0 us)
Sparse Core Ops, SparseCore 0:
  9.6 52.6 all-gather.3
  84.8 84.0 reduce-scatter.18
  172.6 55.8 all-gather.5
  230.7 35.1 reduce-scatter.14
  268.6 92.7 reduce-scatter.20
  363.6 36.3 reduce-scatter.16
  402.1 58.8 all-gather.7
  463.3 35.1 reduce-scatter.22
  501.3 95.2 reduce-scatter.26
  598.7 27.2 reduce-scatter.30
  628.3 33.0 reduce-scatter.24
  663.5 19.2 reduce-scatter.32
  693.4 48.9 reduce-scatter.28
  748.7 189.8 all-reduce.4
